TPU v7x, 32 devices: a whole 2x2x4 slice. The times are simulated.
32 devices in a mesh: section: 4 (over z), dp: 4 (over y, x), tensor: 2 (over core).
Axes of the slice: x: 2, y: 2, z: 4, core: 2. Of those that a mesh axis runs over, the one named last changes fastest.
Arguments:
- sent_out: bfloat16 [4, 2, 768, 4096], P('section', None, 'dp', 'tensor'), may hold values from -6 to 6
- sent_back: bfloat16 [4, 2, 768, 4096], P('section', None, 'dp', 'tensor'), may hold values from -6 to 6
- sent_grad: bfloat16 [4, 2, 768, 4096], P('section', None, 'dp', 'tensor'), may hold values from -6 to 6
- lengths: int32 [4, 4], P('section', 'dp'), may hold values from 48 to 192
- weight: bfloat16 [4, 4096, 4096], P('section', 'dp', 'tensor'), may hold values from -0.09375 to 0.09375
Outputs:
- emitted: bfloat16 [4, 2, 768, 4096], P('section', None, 'dp', 'tensor')
- rebuilt: bfloat16 [4, 2, 768, 4096], P('section', None, 'dp', 'tensor')
- input_grad: bfloat16 [4, 2, 768, 4096], P('section', None, 'dp', 'tensor')
- weight_grad: bfloat16 [4, 4096, 4096], P('section', 'dp', 'tensor')
All inputs are finite; a program needn't handle non-finite values.
Results may differ from a plain program's by a relative error of at most 0.0075.
Values may be sent and summed in bfloat16 or wider, within the bound.
A program may use at most 128 MiB of HBM per device.

v0:
```python
import jax
import jax.numpy as jnp
from jax import lax
from jax.sharding import PartitionSpec as P


def shifted(block, axis, distance):
    devices = range(lax.axis_size(axis))
    route = [((i - distance) % len(devices), i) for i in devices]
    return lax.ppermute(block, axis, route)


def across_rows(left, right):
    return lax.dot_general(
        left, right, (((0,), (0,)), ((), ())), preferred_element_type=jnp.float32
    )


def slope(hidden):
    sigma = jax.nn.sigmoid(hidden)
    return sigma * (1.0 + hidden * (1.0 - sigma))


def local(sent_out, sent_back, sent_grad, lengths, weight):
    token_rows = sent_out.shape[2]
    local_weight = weight[0]
    whole_weight = lax.all_gather(local_weight, "dp", axis=0, tiled=True)
    inbound = shifted(sent_out, "section", 1)
    upper_in = inbound[0, 0]
    lower_in = inbound[0, 1]
    upper_full = lax.all_gather(upper_in, "tensor", axis=1, tiled=True)
    pre = jnp.dot(upper_full, whole_weight, preferred_element_type=jnp.float32)
    upper_out = (lower_in.astype(jnp.float32) + jax.nn.silu(pre)).astype(jnp.bfloat16)
    emitted = jnp.stack([upper_out, upper_in])[None]
    back, incoming = shifted((sent_back, sent_grad), "section", -1)
    back_upper = back[0, 0]
    back_lower = back[0, 1]
    lower_full = lax.all_gather(back_lower, "tensor", axis=1, tiled=True)
    pre_held = jnp.dot(lower_full, whole_weight, preferred_element_type=jnp.float32)
    rebuilt_lower = (back_upper.astype(jnp.float32) - jax.nn.silu(pre_held)).astype(jnp.bfloat16)
    rebuilt = jnp.stack([back_lower, rebuilt_lower])[None]
    keep = (jnp.arange(token_rows, dtype=jnp.int32) < lengths[0, 0])[:, None]
    zero = jnp.zeros((), jnp.bfloat16)
    dupper = jnp.where(keep, incoming[0, 0], zero)
    dlower = jnp.where(keep, incoming[0, 1], zero)
    hidden = (dupper.astype(jnp.float32) * slope(pre_held)).astype(jnp.bfloat16)
    terms = lax.dot_general(
        hidden, whole_weight, (((1,), (1,)), ((), ())), preferred_element_type=jnp.float32
    )
    through = lax.psum_scatter(
        terms.astype(jnp.bfloat16), "tensor", scatter_dimension=1, tiled=True
    ).astype(jnp.float32)
    dupper_in = (dlower.astype(jnp.float32) + through).astype(jnp.bfloat16)
    grads_out = jnp.stack([dupper_in, dupper])[None]
    held_share = lax.all_to_all(lower_full, "dp", split_axis=1, concat_axis=0, tiled=True)
    hidden_all = lax.all_gather(hidden, "dp", axis=0, tiled=True)
    weight_grad = across_rows(held_share, hidden_all).astype(jnp.bfloat16)[None]
    rebuilt, grads_out, weight_grad = (rebuilt, grads_out, weight_grad)
    return (emitted, rebuilt, grads_out, weight_grad)


def solution(mesh):
    return jax.shard_map(
        local,
        mesh=mesh,
        in_specs=(
            P("section", None, "dp", "tensor"),
            P("section", None, "dp", "tensor"),
            P("section", None, "dp", "tensor"),
            P("section", "dp"),
            P("section", "dp", "tensor"),
        ),
        out_specs=(
            P("section", None, "dp", "tensor"),
            P("section", None, "dp", "tensor"),
            P("section", None, "dp", "tensor"),
            P("section", "dp", "tensor"),
        ),
        check_vma=False,
    )
```

profile of v0, /device:TPU:0, one launch (start us, length us, event | category | flops | bytes accessed | tf_op | source)
XLA Modules:
  0.0 327.9 jit_solution(17365934528555776995)
XLA Ops:
  7.2 0.0 all-gather.14.cloned.1.call-start
  7.2 5.1 %collective-permute-start.1 = (bf16[1,2,192,2048]{3,2,1,0:T(8,128)(2,1)}, bf16[1,2,192,2048]{3,2,1,0:T(8,128)(2,1)S(1)}, u32[]{:S(2)}, u32[]{:S(2)}) collective-permute-start(bf16[1,2,192,2048]{3,2,1,0:T(8,128)(2,1)} %param.6), channel_id=1, source_target_pairs={{8,0},{16,8},{24,16},{0,24},{9,1},{17,9},{25,17},{1,25},{10,2},{18... | collective-permute-start | bytes 4718600 | tf_op jit(solution)/shard_map/ppermute | solution.py:10
  12.3 34.0 %collective-permute-done.1 = bf16[1,2,192,2048]{3,2,1,0:T(8,128)(2,1)S(1)} collective-permute-done((bf16[1,2,192,2048]{3,2,1,0:T(8,128)(2,1)}, bf16[1,2,192,2048]{3,2,1,0:T(8,128)(2,1)S(1)}, u32[]{:S(2)}, u32[]{:S(2)}) %collective-permute-start.1) | collective-permute-done | bytes 1572896 | tf_op jit(solution)/shard_map/ppermute | solution.py:10
  46.3 0.0 copy-start.5
  46.3 1.1 copy-done.5
  47.5 1.1 slice_bitcast_fusion.3
  48.5 0.0 all-gather.14.cloned.1.call-update
  48.5 0.0 all-gather.12.cloned.1.call-start
  48.6 0.7 all-gather.12.cloned.1.call-update
  49.3 0.0 all-gather.10.cloned.1.call-start
  49.3 0.4 collective-permute-start
  49.7 3.9 %collective-permute-start.2 = (bf16[1,2,192,2048]{3,2,1,0:T(8,128)(2,1)}, bf16[1,2,192,2048]{3,2,1,0:T(8,128)(2,1)S(1)}, u32[]{:S(2)}, u32[]{:S(2)}) collective-permute-start(bf16[1,2,192,2048]{3,2,1,0:T(8,128)(2,1)} %param.7), channel_id=1, source_target_pairs={{8,0},{16,8},{24,16},{0,24},{9,1},{17,9},{25,17},{1,25},{10,2},{18... | collective-permute-start | bytes 4718600 | tf_op jit(solution)/shard_map/ppermute | solution.py:10
  54.3 34.9 %collective-permute-done = bf16[1,2,192,2048]{3,2,1,0:T(8,128)(2,1)} collective-permute-done((bf16[1,2,192,2048]{3,2,1,0:T(8,128)(2,1)}, bf16[1,2,192,2048]{3,2,1,0:T(8,128)(2,1)}, u32[]{:S(2)}, u32[]{:S(2)}) %collective-permute-start) | collective-permute-done | bytes 1572896 | tf_op jit(solution)/shard_map/ppermute | solution.py:10
  89.2 2.5 fusion.17
  91.7 0.0 all-gather.10.cloned.1.call-update
  91.7 0.0 reduce-scatter.2.cloned.1.call-start
  91.7 26.9 %collective-permute-done.2 = bf16[1,2,192,2048]{3,2,1,0:T(8,128)(2,1)S(1)} collective-permute-done((bf16[1,2,192,2048]{3,2,1,0:T(8,128)(2,1)}, bf16[1,2,192,2048]{3,2,1,0:T(8,128)(2,1)S(1)}, u32[]{:S(2)}, u32[]{:S(2)}) %collective-permute-start.2) | collective-permute-done | bytes 1572896 | tf_op jit(solution)/shard_map/ppermute | solution.py:10
  118.7 0.0 copy-start.1
  118.7 0.0 all-gather.14.cloned.1.call-done
  118.7 102.0 %all-gather.12.cloned.1.call-done = bf16[1,4096,2048]{2,1,0:T(8,128)(2,1)} async-done(((bf16[1,1024,2048]{2,1,0:T(8,128)(2,1)}), bf16[1,4096,2048]{2,1,0:T(8,128)(2,1)}) %all-gather.12.cloned.1.call-update) | async-done | bytes 16777232 | tf_op jit(solution)/shard_map/all_gather | solution.py:27
  220.7 11.4 %multiply_convert_fusion = (bf16[192,2048]{1,0:T(8,128)(2,1)S(1)}, bf16[1,192,2048]{2,1,0:T(8,128)(2,1)}) fusion(pred[192]{0:T(512)(128)(4,1)S(1)} %iota_compare_fusion, bf16[1,2,192,2048]{3,2,1,0:T(8,128)(2,1)S(1)} %collective-permute-done.2, bf16[1,2,192,2048]{3,2,1,0:T(8,128)(2,1)} %copy-done.5, ...), kind=kOutput, calls=%fused_computation.18 | convolution fusion | flops 3227123712 | bytes 21496000 | tf_op jit(solution)/shard_map/dot_general | solution.py:39
  232.0 0.0 copy-start.3
  232.0 12.8 %fusion.6 = bf16[192,4096]{1,0:T(8,128)(2,1)} fusion(bf16[192,2048]{1,0:T(8,128)(2,1)S(1)} %get-tuple-element.12, bf16[1,4096,2048]{2,1,0:T(8,128)(2,1)} %all-gather.12.cloned.1.call-done), kind=kOutput, calls=%fused_computation.6 | convolution fusion | flops 3222011904 | bytes 19136512 | tf_op jit(solution)/shard_map/dot_general | solution.py:47
  244.9 0.0 copy-done.3
  244.9 0.0 reduce-scatter.2.cloned.1.call-update
  244.9 0.0 all-gather.8.cloned.1.call-start
  244.9 0.5 all-gather.8.cloned.1.call-update
  245.5 0.0 copy-done.1
  245.5 0.1 bitcast_select_fusion
  245.6 2.9 all_to_all.14
  248.5 1.7 copy.10
  250.2 4.5 %all-to-all-start = ((bf16[192,4,1024]{2,0,1:T(8,128)(2,1)}), bf16[192,4,1024]{2,0,1:T(8,128)(2,1)}, u32[]{:S(2)}, u32[]{:S(2)}) async-start(bf16[192,4,1024]{2,0,1:T(8,128)(2,1)} %copy.10), calls=%async_computation.1 | async-start | bytes 3145728 | tf_op jit(solution)/shard_map/all_to_all | solution.py:55
  254.8 0.0 copy-start
  254.8 0.0 all-gather.10.cloned.1.call-done
  254.8 10.0 %fusion.15 = bf16[1,192,2048]{2,1,0:T(8,128)(2,1)S(1)} fusion(bf16[1,2,192,2048]{3,2,1,0:T(8,128)(2,1)} %collective-permute-done, bf16[1,4096,2048]{2,1,0:T(8,128)(2,1)} %all-gather.12.cloned.1.call-done, bf16[1,1,192,4096]{3,2,1,0:T(8,128)(2,1)} %all-gather.10.cloned.1.call-done), kind=kOutput, calls=%fused_computation.27 | convolution fusion | flops 3223977984 | bytes 19922944 | tf_op jit(solution)/shard_map/dot_general | solution.py:32
  264.8 0.0 copy-done
  264.8 0.0 copy-start.4
  264.9 1.3 maximum_bitcast_fusion
  266.1 0.1 copy-done.4
  266.2 0.0 copy-start.2
  266.2 1.3 maximum_bitcast_fusion.1
  267.5 0.7 copy-done.2
  268.2 1.4 fusion.13
  269.6 1.3 maximum_bitcast_fusion.2
  270.9 11.0 %all-to-all-done = bf16[192,4,1024]{2,0,1:T(8,128)(2,1)} async-done(((bf16[192,4,1024]{2,0,1:T(8,128)(2,1)}), bf16[192,4,1024]{2,0,1:T(8,128)(2,1)}, u32[]{:S(2)}, u32[]{:S(2)}) %all-to-all-start) | async-done | bytes 1572896 | tf_op jit(solution)/shard_map/all_to_all | solution.py:55
  281.9 25.3 %all-gather.8.cloned.1.call-done = bf16[768,2048]{1,0:T(8,128)(2,1)} async-done(((bf16[192,2048]{1,0:T(8,128)(2,1)}), bf16[768,2048]{1,0:T(8,128)(2,1)}) %all-gather.8.cloned.1.call-update) | async-done | bytes 3145744 | tf_op jit(solution)/shard_map/all_gather | solution.py:56
  307.2 7.8 %convert_bitcast_fusion = bf16[1,1024,2048]{1,2,0:T(8,128)(2,1)} fusion(bf16[768,2048]{1,0:T(8,128)(2,1)} %all-gather.8.cloned.1.call-done, bf16[768,1024]{1,0:T(8,128)(2,1)} %bitcast.18), kind=kOutput, calls=%fused_computation.7 | convolution fusion | flops 3223322624 | bytes 8912896 | tf_op jit(solution)/shard_map/dot_general | solution.py:14
  314.9 6.4 %copy.11 = bf16[1,1024,2048]{2,1,0:T(8,128)(2,1)} copy(bf16[1,1024,2048]{1,2,0:T(8,128)(2,1)} %convert_bitcast_fusion) | data formatting | bytes 8388608
  (2 shorter events, 0.0 us)
Async XLA Ops:
  7.2 111.5 %all-gather.14.cloned.1.call-start = ((), (), s32[]{:S(2)}) async-start(), calls=%async_computation.6 | async-start | bytes 2359296 | tf_op jit(solution)/shard_map/all_gather | solution.py:38
  7.2 39.1 %collective-permute-start.1 = (bf16[1,2,192,2048]{3,2,1,0:T(8,128)(2,1)}, bf16[1,2,192,2048]{3,2,1,0:T(8,128)(2,1)S(1)}, u32[]{:S(2)}, u32[]{:S(2)}) collective-permute-start(bf16[1,2,192,2048]{3,2,1,0:T(8,128)(2,1)} %param.6), channel_id=1, source_target_pairs={{8,0},{16,8},{24,16},{0,24},{9,1},{17,9},{25,17},{1,25},{10,2},{18... | collective-permute-start | bytes 4718600 | tf_op jit(solution)/shard_map/ppermute | solution.py:10
  46.3 1.1 copy-start.5
  48.5 172.1 %all-gather.12.cloned.1.call-start = ((), (), s32[]{:S(2)}) async-start(), calls=%async_computation.5 | async-start | bytes 20971520 | tf_op jit(solution)/shard_map/all_gather | solution.py:27
  49.3 205.5 %all-gather.10.cloned.1.call-start = ((), (), s32[]{:S(2)}) async-start(), calls=%async_computation.4 | async-start | bytes 2359296 | tf_op jit(solution)/shard_map/all_gather | solution.py:31
  49.3 39.8 %collective-permute-start = (bf16[1,2,192,2048]{3,2,1,0:T(8,128)(2,1)}, bf16[1,2,192,2048]{3,2,1,0:T(8,128)(2,1)}, u32[]{:S(2)}, u32[]{:S(2)}) collective-permute-start(bf16[1,2,192,2048]{3,2,1,0:T(8,128)(2,1)} %param.5), channel_id=1, source_target_pairs={{24,0},{0,8},{8,16},{16,24},{25,1},{1,9},{9,17},{17,25},{26,2},{2,... | collective-permute-start | bytes 4718600 | tf_op jit(solution)/shard_map/ppermute | solution.py:10
  49.7 68.9 %collective-permute-start.2 = (bf16[1,2,192,2048]{3,2,1,0:T(8,128)(2,1)}, bf16[1,2,192,2048]{3,2,1,0:T(8,128)(2,1)S(1)}, u32[]{:S(2)}, u32[]{:S(2)}) collective-permute-start(bf16[1,2,192,2048]{3,2,1,0:T(8,128)(2,1)} %param.7), channel_id=1, source_target_pairs={{8,0},{16,8},{24,16},{0,24},{9,1},{17,9},{25,17},{1,25},{10,2},{18... | collective-permute-start | bytes 4718600 | tf_op jit(solution)/shard_map/ppermute | solution.py:10
  91.7 175.8 %reduce-scatter.2.cloned.1.call-start = ((), (), s32[]{:S(2)}) async-start(), calls=%async_computation.2 | async-start | bytes 2359296 | tf_op jit(solution)/shard_map/reduce_scatter | solution.py:50
  118.7 126.8 %copy-start.1 = (bf16[1,2,192,2048]{3,2,1,0:T(8,128)(2,1)}, bf16[1,2,192,2048]{3,2,1,0:T(8,128)(2,1)S(1)}, u32[]{:S(2)}) copy-start(bf16[1,2,192,2048]{3,2,1,0:T(8,128)(2,1)S(1)} %collective-permute-done.2) | copy-start | bytes 4718596
  232.0 12.8 %copy-start.3 = (bf16[192,2048]{1,0:T(8,128)(2,1)}, bf16[192,2048]{1,0:T(8,128)(2,1)S(1)}, u32[]{:S(2)}) copy-start(bf16[192,2048]{1,0:T(8,128)(2,1)S(1)} %get-tuple-element.12) | copy-start | bytes 2359300
  244.9 62.3 %all-gather.8.cloned.1.call-start = ((), (), s32[]{:S(2)}) async-start(), calls=%async_computation.3 | async-start | bytes 3932160 | tf_op jit(solution)/shard_map/all_gather | solution.py:56
  250.2 31.6 %all-to-all-start = ((bf16[192,4,1024]{2,0,1:T(8,128)(2,1)}), bf16[192,4,1024]{2,0,1:T(8,128)(2,1)}, u32[]{:S(2)}, u32[]{:S(2)}) async-start(bf16[192,4,1024]{2,0,1:T(8,128)(2,1)} %copy.10), calls=%async_computation.1 | async-start | bytes 3145728 | tf_op jit(solution)/shard_map/all_to_all | solution.py:55
  254.8 10.0 %copy-start = (bf16[1,192,2048]{2,1,0:T(8,128)(2,1)S(1)}, bf16[1,192,2048]{2,1,0:T(8,128)(2,1)}, u32[]{:S(2)}) copy-start(bf16[1,192,2048]{2,1,0:T(8,128)(2,1)} %get-tuple-element.17) | copy-start | bytes 2359300
  264.8 1.4 copy-start.4
  266.2 2.0 copy-start.2
Sparse Core Ops, SparseCore 0:
  48.7 11.6 all-gather.13
  62.2 158.4 all-gather.11
  222.8 9.7 all-gather.9
  245.0 8.9 reduce-scatter.1
  255.7 51.4 all-gather.7
where the time goes:
time: 329 us; the launch traced here: 328 us
  waiting for transfers between devices  235 us (71%)
  matrix products  42 us (13%)
  local copies, waits for them, and re-layouts  16.5 us (5%)
  between operations  14.5 us (4%)
  starting transfers between devices  14.2 us (4%)
  other arithmetic  5.4 us (2%)
    all_gather x1, waiting for transfers between devices, local(): whole_weight = lax.all_gather(local_weight, 'dp', axis=0, tiled=True)  102 us
    ppermute x3, waiting for transfers between devices, shifted(): return lax.ppermute(block, axis, route)  95.8 us
    all_gather x1, waiting for transfers between devices, local(): hidden_all = lax.all_gather(hidden, 'dp', axis=0, tiled=True)  25.3 us
    dot_general x1, matrix products, local(): lax.dot_general(hidden, whole_weight, (((1,), (1,)), ((), ())), preferred...  12.8 us
    dot_general x1, matrix products, local(): jnp.dot(lower_full, whole_weight, preferred_element_type=jnp.float32)  11.4 us
    all_to_all x1, waiting for transfers between devices, local(): lax.all_to_all(lower_full, 'dp', split_axis=1, concat_axis=0, tiled=True)  11 us
    dot_general x1, matrix products, local(): pre = jnp.dot(upper_full, whole_weight, preferred_element_type=jnp.float32)  9.98 us
    ppermute x3, starting transfers between devices, shifted(): return lax.ppermute(block, axis, route)  9.43 us
  transfers between devices with their start and end apart: 9, of which 6 were waited for; matrix products, arithmetic and copies ran while one was open for 13% of the time, Pallas kernels for 0%

commit v1 on v0

--- a/solution.py
+++ b/solution.py
@@ -53,7 +53,12 @@
     dupper_in = (dlower.astype(jnp.float32) + through).astype(jnp.bfloat16)
     grads_out = jnp.stack([dupper_in, dupper])[None]
     held_share = lax.all_to_all(lower_full, "dp", split_axis=1, concat_axis=0, tiled=True)
-    hidden_all = lax.all_gather(hidden, "dp", axis=0, tiled=True)
+    ring = [hidden]
+    for hop in range(3):
+        ring.append(lax.ppermute(ring[-1], "dp", [(dev, (dev + 1) % 4) for dev in range(4)]))
+    hidden_all = jnp.roll(
+        jnp.concatenate(ring[::-1], axis=0), (lax.axis_index("dp") + 1) * ring[0].shape[0], axis=0
+    )
     weight_grad = across_rows(held_share, hidden_all).astype(jnp.bfloat16)[None]
     rebuilt, grads_out, weight_grad = (rebuilt, grads_out, weight_grad)
     return (emitted, rebuilt, grads_out, weight_grad)

time: 329 us -> 337 us (1.024)
  local copies, waits for them, and re-layouts: 16.5 us -> 24.9 us
    ppermute x0 -> x3, waiting for transfers between devices: none -> 32.2 us  [local(): lax.ppermute(ring[-1], 'dp', [(dev, (dev + 1) % 4) for dev in range(4)])]
    all_gather x1, waiting for transfers between devices: 102 us -> 132 us  [local(): whole_weight = lax.all_gather(local_weight, 'dp', axis=0, tiled=True)]
    ppermute x3, waiting for transfers between devices: 95.8 us -> 68.1 us  [shifted(): return lax.ppermute(block, axis, route)]
    all_gather x1 -> x0, waiting for transfers between devices: 25.3 us -> none  [local(): hidden_all = lax.all_gather(hidden, 'dp', axis=0, tiled=True)]
    all_to_all x1, waiting for transfers between devices: 11 us -> 0.01 us  [local(): lax.all_to_all(lower_full, 'dp', split_axis=1, concat_axis=0, tiled=True)]
    unnamed x13 -> x24, local copies, waits for them, and re-layouts: 8.36 us -> 15.6 us
  transfers between devices with their start and end apart: 9 -> 11, of which waited for: 6 -> 6; matrix products, arithmetic and copies ran while one was open for 13% -> 19% of each run, Pallas kernels for 0% -> 0%
where the time goes in v1:
time: 337 us
  waiting for transfers between devices  233 us (69%)
  matrix products  41.8 us (12%)
  local copies, waits for them, and re-layouts  24.9 us (7%)
  starting transfers between devices  16.3 us (5%)
  between operations  14.5 us (4%)
  other arithmetic  6.37 us (2%)
    all_gather x1, waiting for transfers between devices, local(): whole_weight = lax.all_gather(local_weight, 'dp', axis=0, tiled=True)  132 us
    ppermute x3, waiting for transfers between devices, shifted(): return lax.ppermute(block, axis, route)  68.1 us
    ppermute x3, waiting for transfers between devices, local(): lax.ppermute(ring[-1], 'dp', [(dev, (dev + 1) % 4) for dev in range(4)])  32.2 us
    unnamed x24, local copies, waits for them, and re-layouts  15.6 us
    dot_general x1, matrix products, local(): lax.dot_general(hidden, whole_weight, (((1,), (1,)), ((), ())), preferred...  12.6 us
    dot_general x1, matrix products, local(): jnp.dot(lower_full, whole_weight, preferred_element_type=jnp.float32)  11.4 us
    dot_general x1, matrix products, local(): pre = jnp.dot(upper_full, whole_weight, preferred_element_type=jnp.float32)  9.98 us
    ppermute x3, starting transfers between devices, shifted(): return lax.ppermute(block, axis, route)  9.31 us
  transfers between devices with their start and end apart: 11, of which 6 were waited for; matrix products, arithmetic and copies ran while one was open for 19% of the time, Pallas kernels for 0%

profile of v1, /device:TPU:0, one launch (start us, length us, event | category | flops | bytes accessed | tf_op | source)
XLA Modules:
  0.0 336.7 jit_solution(4016009844788604710)
XLA Ops:
  7.2 0.0 all-gather.11.cloned.1.call-start
  7.2 5.1 %collective-permute-start.1 = (bf16[1,2,192,2048]{3,2,1,0:T(8,128)(2,1)}, bf16[1,2,192,2048]{3,2,1,0:T(8,128)(2,1)S(1)}, u32[]{:S(2)}, u32[]{:S(2)}) collective-permute-start(bf16[1,2,192,2048]{3,2,1,0:T(8,128)(2,1)} %param.6), channel_id=1, source_target_pairs={{8,0},{16,8},{24,16},{0,24},{9,1},{17,9},{25,17},{1,25},{10,2},{18... | collective-permute-start | bytes 4718600 | tf_op jit(solution)/shard_map/ppermute | solution.py:10
  12.3 34.0 %collective-permute-done.1 = bf16[1,2,192,2048]{3,2,1,0:T(8,128)(2,1)S(1)} collective-permute-done((bf16[1,2,192,2048]{3,2,1,0:T(8,128)(2,1)}, bf16[1,2,192,2048]{3,2,1,0:T(8,128)(2,1)S(1)}, u32[]{:S(2)}, u32[]{:S(2)}) %collective-permute-start.1) | collective-permute-done | bytes 1572896 | tf_op jit(solution)/shard_map/ppermute | solution.py:10
  46.3 1.1 copy-done.6
  47.5 1.4 slice_bitcast_fusion.3
  48.8 0.0 all-gather.11.cloned.1.call-update
  48.9 0.0 copy-start.7
  48.9 0.0 all-gather.9.cloned.1.call-start
  48.9 0.7 all-gather.9.cloned.1.call-update
  49.6 0.0 all-gather.7.cloned.1.call-start
  49.7 0.6 copy-done.7
  50.3 4.2 %collective-permute-start.2 = (bf16[1,2,192,2048]{3,2,1,0:T(8,128)(2,1)S(1)}, bf16[1,2,192,2048]{3,2,1,0:T(8,128)(2,1)S(1)}, u32[]{:S(2)}, u32[]{:S(2)}) collective-permute-start(bf16[1,2,192,2048]{3,2,1,0:T(8,128)(2,1)S(1)} %copy-done.7), channel_id=1, source_target_pairs={{8,0},{16,8},{24,16},{0,24},{9,1},{17,9},{25,17},{1,25},{10,2},{18... | collective-permute-start | bytes 4718600 | tf_op jit(solution)/shard_map/ppermute | solution.py:10
  54.4 0.0 collective-permute-start
  55.1 34.1 %collective-permute-done.2 = bf16[1,2,192,2048]{3,2,1,0:T(8,128)(2,1)S(1)} collective-permute-done((bf16[1,2,192,2048]{3,2,1,0:T(8,128)(2,1)S(1)}, bf16[1,2,192,2048]{3,2,1,0:T(8,128)(2,1)S(1)}, u32[]{:S(2)}, u32[]{:S(2)}) %collective-permute-start.2) | collective-permute-done | bytes 1572896 | tf_op jit(solution)/shard_map/ppermute | solution.py:10
  89.2 131.7 %all-gather.9.cloned.1.call-done = bf16[1,4096,2048]{2,1,0:T(8,128)(2,1)} async-done(((bf16[1,1024,2048]{2,1,0:T(8,128)(2,1)}), bf16[1,4096,2048]{2,1,0:T(8,128)(2,1)}) %all-gather.9.cloned.1.call-update) | async-done | bytes 16777232 | tf_op jit(solution)/shard_map/all_gather | solution.py:27
  221.0 11.4 %multiply_convert_fusion = (bf16[192,2048]{1,0:T(8,128)(2,1)S(1)}, bf16[1,192,2048]{2,1,0:T(8,128)(2,1)}) fusion(pred[192]{0:T(512)(128)(4,1)S(1)} %iota_compare_fusion, bf16[1,2,192,2048]{3,2,1,0:T(8,128)(2,1)S(1)} %collective-permute-done.2, bf16[1,2,192,2048]{3,2,1,0:T(8,128)(2,1)} %copy-done.6, bf16[1,4096,2048]{2,1,0:T(8,128)(2,1)} %all-gather.9.cloned.1.call-done, ...), kind=kOutput, calls=%fused_computation.19 | convolution fusion | flops 3227123712 | bytes 21496000 | tf_op jit(solution)/shard_map/dot_general | solution.py:39
  232.3 1.5 collective-permute-start.3
  233.8 0.0 collective-permute-done
  233.8 2.5 fusion.19
  236.3 0.0 all-gather.7.cloned.1.call-update
  236.3 1.0 bitcast_select_fusion
  237.3 2.9 all_to_all.14
  240.2 1.6 copy.10
  241.8 4.4 %all-to-all-start = ((bf16[192,4,1024]{2,0,1:T(8,128)(2,1)}), bf16[192,4,1024]{2,0,1:T(8,128)(2,1)}, u32[]{:S(2)}, u32[]{:S(2)}) async-start(bf16[192,4,1024]{2,0,1:T(8,128)(2,1)} %copy.10), calls=%async_computation.1 | async-start | bytes 3145728 | tf_op jit(solution)/shard_map/all_to_all | solution.py:55
  246.3 0.0 reduce-scatter.2.cloned.1.call-start
  246.3 7.5 %collective-permute-done.3 = bf16[192,2048]{1,0:T(8,128)(2,1)S(1)} collective-permute-done((bf16[192,2048]{1,0:T(8,128)(2,1)S(1)}, bf16[192,2048]{1,0:T(8,128)(2,1)S(1)}, u32[]{:S(2)}, u32[]{:S(2)}) %collective-permute-start.3) | collective-permute-done | bytes 786464 | tf_op jit(solution)/shard_map/ppermute | solution.py:58
  253.8 0.5 collective-permute-start.4
  254.2 12.6 %fusion.6 = bf16[192,4096]{1,0:T(8,128)(2,1)} fusion(bf16[192,2048]{1,0:T(8,128)(2,1)S(1)} %get-tuple-element.12, bf16[1,4096,2048]{2,1,0:T(8,128)(2,1)} %all-gather.9.cloned.1.call-done), kind=kOutput, calls=%fused_computation.6 | convolution fusion | flops 3222011904 | bytes 19136512 | tf_op jit(solution)/shard_map/dot_general | solution.py:47
  266.8 0.0 reduce-scatter.2.cloned.1.call-update
  266.8 19.3 %collective-permute-done.4 = bf16[192,2048]{1,0:T(8,128)(2,1)S(1)} collective-permute-done((bf16[192,2048]{1,0:T(8,128)(2,1)S(1)}, bf16[192,2048]{1,0:T(8,128)(2,1)S(1)}, u32[]{:S(2)}, u32[]{:S(2)}) %collective-permute-start.4) | collective-permute-done | bytes 786464 | tf_op jit(solution)/shard_map/ppermute | solution.py:58
  286.1 0.5 collective-permute-start.5
  286.6 10.0 %fusion.16 = bf16[1,192,2048]{2,1,0:T(8,128)(2,1)S(1)} fusion(bf16[1,2,192,2048]{3,2,1,0:T(8,128)(2,1)} %collective-permute-done, bf16[1,4096,2048]{2,1,0:T(8,128)(2,1)} %all-gather.9.cloned.1.call-done, bf16[1,1,192,4096]{3,2,1,0:T(8,128)(2,1)} %all-gather.7.cloned.1.call-done), kind=kOutput, calls=%fused_computation.28 | convolution fusion | flops 3223977984 | bytes 19922944 | tf_op jit(solution)/shard_map/dot_general | solution.py:32
  296.7 1.3 maximum_bitcast_fusion
  298.0 0.6 copy-done.5
  298.6 1.3 maximum_bitcast_fusion.1
  299.9 5.4 %collective-permute-done.5 = bf16[192,2048]{1,0:T(8,128)(2,1)S(1)} collective-permute-done((bf16[192,2048]{1,0:T(8,128)(2,1)S(1)}, bf16[192,2048]{1,0:T(8,128)(2,1)S(1)}, u32[]{:S(2)}, u32[]{:S(2)}) %collective-permute-start.5) | collective-permute-done | bytes 786464 | tf_op jit(solution)/shard_map/ppermute | solution.py:58
  305.3 0.9 constant_dynamic-update-slice_fusion.7
  306.2 1.0 constant_dynamic-update-slice_fusion.6
  307.2 1.0 constant_dynamic-update-slice_fusion.5
  308.2 0.9 constant_dynamic-update-slice_fusion.4
  309.1 0.9 constant_dynamic-update-slice_fusion.3
  310.0 0.9 constant_dynamic-update-slice_fusion.2
  311.0 1.0 constant_dynamic-update-slice_fusion.1
  312.0 0.9 constant_dynamic-update-slice_fusion
  312.9 7.9 %convert_bitcast_fusion = bf16[1,1024,2048]{1,2,0:T(8,128)(2,1)} fusion(bf16[768,1024]{1,0:T(8,128)(2,1)} %bitcast.18, bf16[1536,2048]{1,0:T(8,128)(2,1)} %constant_dynamic-update-slice_fusion, s32[]{:T(128)S(6)} %select_n.33), kind=kOutput, calls=%fused_computation.7 | convolution fusion | flops 3223322624 | bytes 8912900 | tf_op jit(solution)/shard_map/dot_general | solution.py:14
  320.8 6.5 %copy.11 = bf16[1,1024,2048]{2,1,0:T(8,128)(2,1)} copy(bf16[1,1024,2048]{1,2,0:T(8,128)(2,1)} %convert_bitcast_fusion) | data formatting | bytes 8388608
  327.4 1.5 fusion.14
  328.9 1.3 maximum_bitcast_fusion.2
  (17 shorter events, 0.0 us)
Async XLA Ops:
  7.2 82.1 %all-gather.11.cloned.1.call-start = ((), (), s32[]{:S(2)}) async-start(), calls=%async_computation.5 | async-start | bytes 2359296 | tf_op jit(solution)/shard_map/all_gather | solution.py:38
  7.2 39.1 %collective-permute-start.1 = (bf16[1,2,192,2048]{3,2,1,0:T(8,128)(2,1)}, bf16[1,2,192,2048]{3,2,1,0:T(8,128)(2,1)S(1)}, u32[]{:S(2)}, u32[]{:S(2)}) collective-permute-start(bf16[1,2,192,2048]{3,2,1,0:T(8,128)(2,1)} %param.6), channel_id=1, source_target_pairs={{8,0},{16,8},{24,16},{0,24},{9,1},{17,9},{25,17},{1,25},{10,2},{18... | collective-permute-start | bytes 4718600 | tf_op jit(solution)/shard_map/ppermute | solution.py:10
  46.3 1.1 copy-start.6
  48.9 1.4 copy-start.7
  48.9 172.1 %all-gather.9.cloned.1.call-start = ((), (), s32[]{:S(2)}) async-start(), calls=%async_computation.4 | async-start | bytes 20971520 | tf_op jit(solution)/shard_map/all_gather | solution.py:27
  49.6 237.0 %all-gather.7.cloned.1.call-start = ((), (), s32[]{:S(2)}) async-start(), calls=%async_computation.3 | async-start | bytes 2359296 | tf_op jit(solution)/shard_map/all_gather | solution.py:31
  50.3 39.0 %collective-permute-start.2 = (bf16[1,2,192,2048]{3,2,1,0:T(8,128)(2,1)S(1)}, bf16[1,2,192,2048]{3,2,1,0:T(8,128)(2,1)S(1)}, u32[]{:S(2)}, u32[]{:S(2)}) collective-permute-start(bf16[1,2,192,2048]{3,2,1,0:T(8,128)(2,1)S(1)} %copy-done.7), channel_id=1, source_target_pairs={{8,0},{16,8},{24,16},{0,24},{9,1},{17,9},{25,17},{1,25},{10,2},{18... | collective-permute-start | bytes 4718600 | tf_op jit(solution)/shard_map/ppermute | solution.py:10
  54.4 179.4 %collective-permute-start = (bf16[1,2,192,2048]{3,2,1,0:T(8,128)(2,1)}, bf16[1,2,192,2048]{3,2,1,0:T(8,128)(2,1)}, u32[]{:S(2)}, u32[]{:S(2)}) collective-permute-start(bf16[1,2,192,2048]{3,2,1,0:T(8,128)(2,1)} %param.5), channel_id=1, source_target_pairs={{24,0},{0,8},{8,16},{16,24},{25,1},{1,9},{9,17},{17,25},{26,2},{2,... | collective-permute-start | bytes 4718600 | tf_op jit(solution)/shard_map/ppermute | solution.py:10
  89.2 147.1 %copy-start.3 = (bf16[1,2,192,2048]{3,2,1,0:T(8,128)(2,1)}, bf16[1,2,192,2048]{3,2,1,0:T(8,128)(2,1)S(1)}, u32[]{:S(2)}) copy-start(bf16[1,2,192,2048]{3,2,1,0:T(8,128)(2,1)S(1)} %collective-permute-done.2) | copy-start | bytes 4718596
  232.3 21.4 %collective-permute-start.3 = (bf16[192,2048]{1,0:T(8,128)(2,1)S(1)}, bf16[192,2048]{1,0:T(8,128)(2,1)S(1)}, u32[]{:S(2)}, u32[]{:S(2)}) collective-permute-start(bf16[192,2048]{1,0:T(8,128)(2,1)S(1)} %get-tuple-element.12), channel_id=1, source_target_pairs={{0,2},{2,4},{4,6},{6,0},{1,3},{3,5},{5,7},{7,1},{8,10},{10,12},{12... | collective-permute-start | bytes 2359304 | tf_op jit(solution)/shard_map/ppermute | solution.py:58
  241.8 71.1 %all-to-all-start = ((bf16[192,4,1024]{2,0,1:T(8,128)(2,1)}), bf16[192,4,1024]{2,0,1:T(8,128)(2,1)}, u32[]{:S(2)}, u32[]{:S(2)}) async-start(bf16[192,4,1024]{2,0,1:T(8,128)(2,1)} %copy.10), calls=%async_computation.1 | async-start | bytes 3145728 | tf_op jit(solution)/shard_map/all_to_all | solution.py:55
  246.3 81.1 %reduce-scatter.2.cloned.1.call-start = ((), (), s32[]{:S(2)}) async-start(), calls=%async_computation.2 | async-start | bytes 2359296 | tf_op jit(solution)/shard_map/reduce_scatter | solution.py:50
  253.8 32.4 %collective-permute-start.4 = (bf16[192,2048]{1,0:T(8,128)(2,1)S(1)}, bf16[192,2048]{1,0:T(8,128)(2,1)S(1)}, u32[]{:S(2)}, u32[]{:S(2)}) collective-permute-start(bf16[192,2048]{1,0:T(8,128)(2,1)S(1)} %collective-permute-done.3), channel_id=1, source_target_pairs={{0,2},{2,4},{4,6},{6,0},{1,3},{3,5},{5,7},{7,1},{8,10},{10,12},{12... | collective-permute-start | bytes 2359304 | tf_op jit(solution)/shard_map/ppermute | solution.py:58
  286.1 19.2 %collective-permute-start.5 = (bf16[192,2048]{1,0:T(8,128)(2,1)S(1)}, bf16[192,2048]{1,0:T(8,128)(2,1)S(1)}, u32[]{:S(2)}, u32[]{:S(2)}) collective-permute-start(bf16[192,2048]{1,0:T(8,128)(2,1)S(1)} %collective-permute-done.4), channel_id=1, source_target_pairs={{0,2},{2,4},{4,6},{6,0},{1,3},{3,5},{5,7},{7,1},{8,10},{10,12},{12... | collective-permute-start | bytes 2359304 | tf_op jit(solution)/shard_map/ppermute | solution.py:58
  286.6 10.0 %copy-start.2 = (bf16[1,192,2048]{2,1,0:T(8,128)(2,1)S(1)}, bf16[1,192,2048]{2,1,0:T(8,128)(2,1)}, u32[]{:S(2)}) copy-start(bf16[1,192,2048]{2,1,0:T(8,128)(2,1)} %get-tuple-element.17) | copy-start | bytes 2359300
  296.6 1.3 copy-start.1
  296.7 1.9 copy-start.5
  320.8 6.5 %copy-start.4 = (bf16[1,2,192,2048]{3,2,1,0:T(8,128)(2,1)S(1)}, bf16[1,2,192,2048]{3,2,1,0:T(8,128)(2,1)}, u32[]{:S(2)}) copy-start(bf16[1,2,192,2048]{3,2,1,0:T(8,128)(2,1)} %copy-done.3) | copy-start | bytes 4718596
  327.4 1.5 copy-start
Sparse Core Ops, SparseCore 0:
  49.0 11.6 all-gather.10
  62.5 158.4 all-gather.8
  236.4 9.7 all-gather.6
  266.9 9.9 reduce-scatter.1
